TPU v7x, 32 devices: a whole 2x2x4 slice. The times are simulated.
32 devices in a mesh: seq: 8 (over z, x), head: 4 (over y, core).
Axes of the slice: x: 2, y: 2, z: 4, core: 2. Of those that a mesh axis runs over, the one named last changes fastest.
Arguments:
- block_input: bfloat16 [4096, 2048], P(('seq', 'head')), may hold values from -6 to 6
- norm1_gain: float32 [2048], replicated, may hold values from 0.5 to 1.5
- query_weight: bfloat16 [2048, 2048], P(None, 'head'), may hold values from -0.125 to 0.125
- key_weight: bfloat16 [2048, 2048], P(None, 'head'), may hold values from -0.125 to 0.125
- value_weight: bfloat16 [2048, 2048], P(None, 'head'), may hold values from -0.125 to 0.125
- gate_weight: bfloat16 [2048, 2048], P(None, 'head'), may hold values from -0.125 to 0.125
- rate_weight: bfloat16 [2048, 32], P(None, 'head'), may hold values from -0.125 to 0.125
- rate_bias: float32 [32], P('head'), may hold values from -3 to 3
- rate_scale: float32 [32], P('head'), may hold values from 7.324219e-05 to 0.008
- init_state: float32 [32, 64, 64], P('head'), may hold values from -0.75 to 0.75
- init_bias: float32 [32, 64], P('head'), may hold values from -5 to 5
- post_gain: float32 [2048], P('head'), may hold values from 0.5 to 1.5
- post_bias: float32 [2048], P('head'), may hold values from -3 to 3
- out_weight: bfloat16 [2048, 2048], P('head'), may hold values from -0.25 to 0.25
- norm2_gain: float32 [2048], replicated, may hold values from 0.5 to 1.5
- mlp_gate: bfloat16 [2048, 5504], P(None, 'head'), may hold values from -0.125 to 0.125
- mlp_up: bfloat16 [2048, 5504], P(None, 'head'), may hold values from -0.125 to 0.125
- mlp_down: bfloat16 [5504, 2048], P('head'), may hold values from -0.15625 to 0.15625
- out_cotangent: bfloat16 [4096, 2048], P(('seq', 'head')), may hold values from -6 to 6
Outputs:
- block_out: bfloat16 [4096, 2048], P(('seq', 'head'))
- input_grad: float32 [4096, 2048], P(('seq', 'head'))
- norm1_gain_grad: float32 [2048], replicated
- query_weight_grad: float32 [2048, 2048], P(None, 'head')
- key_weight_grad: float32 [2048, 2048], P(None, 'head')
- value_weight_grad: float32 [2048, 2048], P(None, 'head')
- gate_weight_grad: float32 [2048, 2048], P(None, 'head')
- rate_weight_grad: float32 [2048, 32], P(None, 'head')
- rate_bias_grad: float32 [32], P('head')
- rate_scale_grad: float32 [32], P('head')
- init_state_grad: float32 [32, 64, 64], P('head')
- init_bias_grad: float32 [32, 64], P('head')
- post_gain_grad: float32 [2048], P('head')
- post_bias_grad: float32 [2048], P('head')
- out_weight_grad: float32 [2048, 2048], P('head')
- norm2_gain_grad: float32 [2048], replicated
- mlp_gate_grad: float32 [2048, 5504], P(None, 'head')
- mlp_up_grad: float32 [2048, 5504], P(None, 'head')
- mlp_down_grad: float32 [5504, 2048], P('head')
All inputs are finite; a program needn't handle non-finite values.
Results may differ from a plain program's by a relative error of at most 0.025.
Values may be sent and summed in bfloat16 or wider, within the bound.
No kernel may reach another device: no remote copies, remote signals or barrier semaphores. Data moves between devices by JAX's collectives and lax.ppermute only.
A program may use at most 256 MiB of HBM per device.

v0:
```python
import jax
import jax.numpy as jnp
from jax import lax
from jax.sharding import PartitionSpec as P

MB = 16
HIGHEST = lax.Precision.HIGHEST
EPSILON = 1e-06


def passed_along(shard, axis, by):
    size = lax.axis_size(axis)
    pairs = [(i, i + by) for i in range(size) if 0 <= i + by < size]
    return lax.ppermute(shard, axis, pairs)


def augment(values):
    ones_col = jnp.ones(values.shape[:-1] + (1,), jnp.float32)
    return jnp.concatenate([values, ones_col], axis=-1)


def compose(earlier, later):
    matrix = jnp.einsum("...ij,...jk->...ik", later[0], earlier[0], precision=HIGHEST)
    offset = jnp.einsum("...ij,...jk->...ik", later[0], earlier[1], precision=HIGHEST) + later[1]
    return (matrix, offset)


def apply_map(matrix, offset, inner_state):
    return jnp.einsum("...ij,...jk->...ik", matrix, inner_state, precision=HIGHEST) + offset


def step_matrix_of(key_block, rate_block):
    key_aug = augment(key_block)
    weighted_keys = key_aug * rate_block[..., None]
    identity = jnp.eye(key_aug.shape[-1], dtype=jnp.float32)
    return (
        identity - jnp.einsum("hni,hnj->hij", weighted_keys, key_aug, precision=HIGHEST),
        weighted_keys,
    )


def segment_map(identity, zero_state, key_blocks, value_blocks, rate_blocks):

    def turn(carry, inputs):
        key_block, value_block, rate_block = inputs
        step_matrix, weighted_keys = step_matrix_of(key_block, rate_block)
        step_offset = jnp.einsum(
            "hni,hno->hio", weighted_keys, value_block - key_block, precision=HIGHEST
        )
        return (compose(carry, (step_matrix, step_offset)), None)

    result, unused = lax.scan(turn, (identity, zero_state), (key_blocks, value_blocks, rate_blocks))
    return result


def causal_weights(query_block, key_block, rate_block):
    query_aug = augment(query_block)
    key_aug = augment(key_block)
    scores = jnp.einsum("hmi,hni->hmn", query_aug, key_aug, precision=HIGHEST)
    causal_mask = jnp.tril(jnp.ones((scores.shape[1], scores.shape[2]), jnp.float32))
    return (query_aug, key_aug, scores * causal_mask * rate_block[:, None, :])


def inner_block(inner_state, inputs):
    query_block, key_block, value_block, rate_block = inputs
    query_aug, key_aug, weighted = causal_weights(query_block, key_block, rate_block)
    errors = jnp.einsum("hmi,hio->hmo", key_aug, inner_state, precision=HIGHEST) - (
        value_block - key_block
    )
    outputs = (
        query_block
        + jnp.einsum("hmi,hio->hmo", query_aug, inner_state, precision=HIGHEST)
        - jnp.einsum("hmn,hno->hmo", weighted, errors, precision=HIGHEST)
    )
    new_state = inner_state - jnp.einsum(
        "hni,hno->hio", key_aug * rate_block[:, :, None], errors, precision=HIGHEST
    )
    return (new_state, outputs)


def segment_run(state_in, query_blocks, key_blocks, value_blocks, rate_blocks):
    last_state, outputs = lax.scan(
        jax.checkpoint(inner_block), state_in, (query_blocks, key_blocks, value_blocks, rate_blocks)
    )
    return (outputs, last_state)


def local_state_grad(zero_state, query_blocks, key_blocks, rate_blocks, d_z_blocks):

    def turn(pending, inputs):
        query_block, key_block, rate_block, d_z_block = inputs
        query_aug, key_aug, weighted = causal_weights(query_block, key_block, rate_block)
        back_errors = jnp.einsum("hmn,hmo->hno", weighted, d_z_block, precision=HIGHEST)
        direct = jnp.einsum("hmi,hmo->hio", query_aug, d_z_block, precision=HIGHEST) - jnp.einsum(
            "hni,hno->hio", key_aug, back_errors, precision=HIGHEST
        )
        step_matrix, unused = step_matrix_of(key_block, rate_block)
        return (jnp.einsum("hji,hjo->hio", step_matrix, pending, precision=HIGHEST) + direct, None)

    result, unused = lax.scan(
        turn, zero_state, (query_blocks, key_blocks, rate_blocks, d_z_blocks), reverse=True
    )
    return result


def to_heads(values, local_heads, head_width):
    return values.reshape(-1, MB, local_heads, head_width).transpose(0, 2, 1, 3)


def from_heads(values):
    block_count, head_count, block_size, head_width = values.shape
    return values.transpose(0, 2, 1, 3).reshape(block_count * block_size, head_count * head_width)


def gelu_tanh(values):
    return jax.nn.gelu(values, approximate=True)


def relay_state(values, offset):
    return passed_along(values, "seq", offset)


def body(
    block_input,
    norm1_gain,
    query_weight,
    key_weight,
    value_weight,
    gate_weight,
    rate_weight,
    rate_bias,
    rate_scale,
    init_state,
    init_bias,
    post_gain,
    post_bias,
    out_weight,
    norm2_gain,
    mlp_gate,
    mlp_up,
    mlp_down,
    out_cotangent,
):
    local_heads = init_state.shape[0]
    head_width = init_state.shape[1]
    model_width = block_input.shape[1]
    seq_index = lax.axis_index("seq")
    seq_count = lax.axis_size("seq")
    input_f32 = block_input.astype(jnp.float32)
    scale_in = lax.rsqrt(jnp.mean(input_f32 * input_f32, axis=-1, keepdims=True) + EPSILON)
    unit_in = input_f32 * scale_in
    normed = (unit_in * norm1_gain).astype(jnp.bfloat16)
    group_in, group_cot = (
        lax.all_gather(normed, "head", axis=0, tiled=True),
        lax.all_gather(out_cotangent, "head", axis=0, tiled=True),
    )
    query_rows = jnp.dot(group_in, query_weight, preferred_element_type=jnp.float32)
    key_rows = jnp.dot(group_in, key_weight, preferred_element_type=jnp.float32)
    value_rows = jnp.dot(group_in, value_weight, preferred_element_type=jnp.float32)
    gate_pre = jnp.dot(group_in, gate_weight, preferred_element_type=jnp.float32)
    rate_pre = jnp.dot(group_in, rate_weight, preferred_element_type=jnp.float32) + rate_bias
    rate_sig = jax.nn.sigmoid(rate_pre)
    rate_rows = rate_sig * rate_scale
    query_blocks = to_heads(query_rows, local_heads, head_width)
    key_blocks = to_heads(key_rows, local_heads, head_width)
    value_blocks = to_heads(value_rows, local_heads, head_width)
    rate_blocks = rate_rows.reshape(-1, MB, local_heads).transpose(0, 2, 1)
    aug_width = head_width + 1
    identity = jnp.broadcast_to(
        jnp.eye(aug_width, dtype=jnp.float32), (local_heads, aug_width, aug_width)
    )
    start_state = jnp.concatenate([init_state, init_bias[:, None, :]], axis=1)
    zero_state = jnp.zeros_like(start_state)
    segment_matrix, segment_offset = segment_map(
        identity, zero_state, key_blocks, value_blocks, rate_blocks
    )

    def forward_turn(turn, incoming):
        received = relay_state(apply_map(segment_matrix, segment_offset, incoming), 1)
        return jnp.where(seq_index == 0, start_state, received)

    state_in = lax.fori_loop(0, seq_count - 1, forward_turn, start_state)
    (z_blocks, last_state), inner_pullback = jax.vjp(
        segment_run, state_in, query_blocks, key_blocks, value_blocks, rate_blocks
    )
    z_rows = from_heads(z_blocks)
    stat_sums = lax.psum((jnp.sum(z_rows, axis=-1), jnp.sum(z_rows * z_rows, axis=-1)), "head")
    row_mean = stat_sums[0] / model_width
    row_var = stat_sums[1] / model_width - row_mean * row_mean
    inv_scale = lax.rsqrt(row_var + EPSILON)[:, None]
    z_hat = (z_rows - row_mean[:, None]) * inv_scale
    post_out = z_hat * post_gain + post_bias
    gate_act, gelu_back = jax.vjp(gelu_tanh, gate_pre)
    gated_out = (gate_act * post_out).astype(jnp.bfloat16)
    picked = gated_out
    attn_out = lax.psum_scatter(
        jnp.dot(picked, out_weight, preferred_element_type=jnp.float32).astype(jnp.bfloat16),
        "head",
        scatter_dimension=0,
        tiled=True,
    ).astype(jnp.float32)
    middle = input_f32 + attn_out
    scale_mid = lax.rsqrt(jnp.mean(middle * middle, axis=-1, keepdims=True) + EPSILON)
    unit_mid = middle * scale_mid
    mlp_input = (unit_mid * norm2_gain).astype(jnp.bfloat16)
    mlp_group = lax.all_gather(mlp_input, "head", axis=0, tiled=True)
    gate_mlp = jnp.dot(mlp_group, mlp_gate, preferred_element_type=jnp.float32)
    up_mlp = jnp.dot(mlp_group, mlp_up, preferred_element_type=jnp.float32)
    silu_gate, silu_back = jax.vjp(jax.nn.silu, gate_mlp)
    hidden = (silu_gate * up_mlp).astype(jnp.bfloat16)
    picked = hidden
    mlp_out = lax.psum_scatter(
        jnp.dot(picked, mlp_down, preferred_element_type=jnp.float32).astype(jnp.bfloat16),
        "head",
        scatter_dimension=0,
        tiled=True,
    ).astype(jnp.float32)
    block_out = (middle + mlp_out).astype(jnp.bfloat16)
    cot_f32 = out_cotangent.astype(jnp.float32)
    d_hidden = jnp.dot(group_cot, mlp_down.T, preferred_element_type=jnp.float32)
    mlp_down_grad = jnp.dot(hidden.T, group_cot, preferred_element_type=jnp.float32)
    d_gate_mlp = silu_back(d_hidden * up_mlp)[0].astype(jnp.bfloat16)
    d_up_mlp = (d_hidden * silu_gate).astype(jnp.bfloat16)
    mlp_gate_grad = jnp.dot(mlp_group.T, d_gate_mlp, preferred_element_type=jnp.float32)
    mlp_up_grad = jnp.dot(mlp_group.T, d_up_mlp, preferred_element_type=jnp.float32)
    d_mlp_input = lax.psum_scatter(
        jnp.dot(d_gate_mlp, mlp_gate.T, preferred_element_type=jnp.float32)
        + jnp.dot(d_up_mlp, mlp_up.T, preferred_element_type=jnp.float32),
        "head",
        scatter_dimension=0,
        tiled=True,
    )
    scaled_mid = d_mlp_input * norm2_gain
    norm2_part = jnp.sum(d_mlp_input * unit_mid, axis=0)
    d_middle = cot_f32 + scale_mid * (
        scaled_mid - unit_mid * jnp.mean(scaled_mid * unit_mid, axis=-1, keepdims=True)
    )
    d_attn = d_middle.astype(jnp.bfloat16)
    d_attn_group = lax.all_gather(d_attn, "head", axis=0, tiled=True)
    d_gated = jnp.dot(d_attn_group, out_weight.T, preferred_element_type=jnp.float32)
    out_weight_grad = jnp.dot(gated_out.T, d_attn_group, preferred_element_type=jnp.float32)
    d_post = d_gated * gate_act
    d_gate_pre = gelu_back(d_gated * post_out)[0].astype(jnp.bfloat16)
    post_gain_part = jnp.sum(d_post * z_hat, axis=0)
    post_bias_part = jnp.sum(d_post, axis=0)
    d_zhat = d_post * post_gain
    back_sums = lax.psum((jnp.sum(d_zhat, axis=-1), jnp.sum(d_zhat * z_hat, axis=-1)), "head")
    d_z = inv_scale * (
        d_zhat - back_sums[0][:, None] / model_width - z_hat * (back_sums[1][:, None] / model_width)
    )
    d_z_blocks = to_heads(d_z, local_heads, head_width)
    local_state = local_state_grad(zero_state, query_blocks, key_blocks, rate_blocks, d_z_blocks)
    back_matrix = jnp.swapaxes(segment_matrix, 1, 2)

    def backward_turn(turn, pending):
        return relay_state(apply_map(back_matrix, local_state, pending), -1)

    grad_out = lax.fori_loop(0, seq_count - 1, backward_turn, zero_state)
    all_terms = inner_pullback((d_z_blocks, grad_out))
    init_part = jnp.where(seq_index == 0, all_terms[0], 0.0)
    d_query = from_heads(all_terms[1]).astype(jnp.bfloat16)
    d_key = from_heads(all_terms[2]).astype(jnp.bfloat16)
    d_value = from_heads(all_terms[3]).astype(jnp.bfloat16)
    d_rate = all_terms[4].transpose(0, 2, 1).reshape(-1, local_heads)
    d_rate_pre = (d_rate * rate_scale * rate_sig * (1.0 - rate_sig)).astype(jnp.bfloat16)
    scale_part = jnp.sum(d_rate * rate_sig, axis=0)
    rate_bias_part = jnp.sum(d_rate_pre.astype(jnp.float32), axis=0)
    query_grad = jnp.dot(group_in.T, d_query, preferred_element_type=jnp.float32)
    key_grad = jnp.dot(group_in.T, d_key, preferred_element_type=jnp.float32)
    value_grad = jnp.dot(group_in.T, d_value, preferred_element_type=jnp.float32)
    gate_grad = jnp.dot(group_in.T, d_gate_pre, preferred_element_type=jnp.float32)
    rate_weight_part = jnp.dot(group_in.T, d_rate_pre, preferred_element_type=jnp.float32)

    def picked(values):
        return values

    total = jnp.dot(picked(d_query), query_weight.T, preferred_element_type=jnp.float32)
    total = total + jnp.dot(picked(d_key), key_weight.T, preferred_element_type=jnp.float32)
    total = total + jnp.dot(picked(d_value), value_weight.T, preferred_element_type=jnp.float32)
    total = total + jnp.dot(picked(d_gate_pre), gate_weight.T, preferred_element_type=jnp.float32)
    d_normed = lax.psum_scatter(
        (
            total + jnp.dot(picked(d_rate_pre), rate_weight.T, preferred_element_type=jnp.float32)
        ).astype(jnp.bfloat16),
        "head",
        scatter_dimension=0,
        tiled=True,
    ).astype(jnp.float32)
    scaled_in = d_normed * norm1_gain
    norm1_part = jnp.sum(d_normed * unit_in, axis=0)
    input_grad = d_middle + scale_in * (
        scaled_in - unit_in * jnp.mean(scaled_in * unit_in, axis=-1, keepdims=True)
    )
    summed = (
        lax.psum(query_grad.astype(jnp.bfloat16), "seq").astype(jnp.float32),
        lax.psum(key_grad.astype(jnp.bfloat16), "seq").astype(jnp.float32),
        lax.psum(value_grad.astype(jnp.bfloat16), "seq").astype(jnp.float32),
        lax.psum(gate_grad.astype(jnp.bfloat16), "seq").astype(jnp.float32),
        lax.psum(rate_weight_part.astype(jnp.bfloat16), "seq").astype(jnp.float32),
        lax.psum(rate_bias_part.astype(jnp.bfloat16), "seq").astype(jnp.float32),
        lax.psum(scale_part.astype(jnp.bfloat16), "seq").astype(jnp.float32),
        lax.psum(init_part.astype(jnp.bfloat16), "seq").astype(jnp.float32),
        lax.psum(post_gain_part.astype(jnp.bfloat16), "seq").astype(jnp.float32),
        lax.psum(post_bias_part.astype(jnp.bfloat16), "seq").astype(jnp.float32),
        lax.psum(out_weight_grad.astype(jnp.bfloat16), "seq").astype(jnp.float32),
        lax.psum(mlp_gate_grad.astype(jnp.bfloat16), "seq").astype(jnp.float32),
        lax.psum(mlp_up_grad.astype(jnp.bfloat16), "seq").astype(jnp.float32),
        lax.psum(mlp_down_grad.astype(jnp.bfloat16), "seq").astype(jnp.float32),
    )
    gain_grads = lax.psum((norm1_part, norm2_part), ("seq", "head"))
    init_total = summed[7]
    return (
        block_out,
        input_grad,
        gain_grads[0],
        summed[0],
        summed[1],
        summed[2],
        summed[3],
        summed[4],
        summed[5],
        summed[6],
        init_total[:, :head_width, :],
        init_total[:, head_width, :],
        summed[8],
        summed[9],
        summed[10],
        gain_grads[1],
        summed[11],
        summed[12],
        summed[13],
    )


def solution(mesh):
    in_specs = (
        P(("seq", "head"), None),
        P(),
        P(None, "head"),
        P(None, "head"),
        P(None, "head"),
        P(None, "head"),
        P(None, "head"),
        P("head"),
        P("head"),
        P("head", None, None),
        P("head", None),
        P("head"),
        P("head"),
        P("head", None),
        P(),
        P(None, "head"),
        P(None, "head"),
        P("head", None),
        P(("seq", "head"), None),
    )
    out_specs = (
        P(("seq", "head"), None),
        P(("seq", "head"), None),
        P(),
        P(None, "head"),
        P(None, "head"),
        P(None, "head"),
        P(None, "head"),
        P(None, "head"),
        P("head"),
        P("head"),
        P("head", None, None),
        P("head", None),
        P("head"),
        P("head"),
        P("head", None),
        P(),
        P(None, "head"),
        P(None, "head"),
        P("head", None),
    )
    return jax.shard_map(body, mesh=mesh, in_specs=in_specs, out_specs=out_specs, check_vma=False)
```

profile of v0, /device:TPU:0, one launch (start us, length us, event | category | flops | bytes accessed | tf_op | source)
XLA Modules:
  0.0 2290.9 jit_solution(17241817064741074859)
XLA Ops:
  11.3 24.8 %all-gather.5.cloned.1.call-done = bf16[512,2048]{1,0:T(8,128)(2,1)} async-done(((bf16[128,2048]{1,0:T(8,128)(2,1)}), bf16[512,2048]{1,0:T(8,128)(2,1)}) %all-gather.5.cloned.1.call-update) | async-done | bytes 2097168 | tf_op jit(solution)/shard_map/all_gather | solution.py:154
  67.1 164.2 %while.97 = (s32[]{:T(128)}, f32[8,65,65]{2,1,0:T(8,128)S(1)}, f32[8,65,64]{1,2,0:T(8,128)S(1)}, f32[32,8,16,64]{3,2,1,0:T(8,128)}, f32[32,8,16]{2,1,0:T(8,128)}, /*index=5*/f32[32,8,16,64]{3,2,1,0:T(8,128)}) while((s32[]{:T(128)}, f32[8,65,65]{2,1,0:T(8,128)S(1)}, f32[8,65,64]{1,2,0:T(8,128)S(1)}, ...), condition=%wide.region_2.3_spmd.clone.clone, body=%wide.region_1.2_spmd.clone.sunk.clone | while | flops 65335404 | bytes 1942347 | solution.py:52
  231.3 75.0 %while.93 = (s32[]{:T(128)}, f32[8,65,64]{1,2,0:T(8,128)S(1)}, pred[]{:T(512)}, f32[8,65,65]{2,1,0:T(8,128)S(1)}, f32[8,65,64]{1,2,0:T(8,128)S(1)}, /*index=5*/f32[8,65,64]{1,2,0:T(8,128)S(1)}) while((s32[]{:T(128)}, f32[8,65,64]{1,2,0:T(8,128)S(1)}, pred[]{:T(512)}, f32[8,65,65]{2,1,0:T(8,128)S(1)}, f32[8,65,64]{1,2,0:T(8,128)S(1)}, ...), condition=%wide.region_4.5_spmd.clone, body=%wide.region_3.4_spmd.sunk.clone | while | flops 26024960 | bytes 1466510 | solution.py:182
  236.0 6.3 collective-permute-done
  306.4 189.6 %while.96 = (s32[]{:T(128)}, f32[8,65,64]{1,2,0:T(8,128)S(1)}, f32[32,8,16,64]{3,2,1,0:T(8,128)}, f32[32,8,65,64]{2,3,1,0:T(8,128)}, f32[32,8,16,64]{3,2,1,0:T(8...) while((s32[]{:T(128)}, f32[8,65,64]{1,2,0:T(8,128)S(1)}, ...), condition=%wide.region_6.7_spmd.clone.clone, body=%wide.region_5.6_spmd.clone.sunk.clone | while | flops 22418560 | bytes 1732721 | solution.py:82
  504.7 6.1 all-reduce.9
  518.4 34.2 %reduce-scatter.5.cloned.1.call-done = bf16[128,2048]{1,0:T(8,128)(2,1)} async-done(((bf16[512,2048]{1,0:T(8,128)(2,1)}), bf16[128,2048]{1,0:T(8,128)(2,1)}) %reduce-scatter.5.cloned.1.call-update) | async-done | bytes 524304 | tf_op jit(solution)/shard_map/reduce_scatter | solution.py:196
  556.6 22.1 all-gather.7.cloned.1.call-done
  578.8 8.1 fusion.139
  586.8 7.7 fusion.138
  594.5 8.4 all-gather.9.cloned.1.call-done
  602.9 10.3 multiply_convert_fusion
  613.1 6.4 fusion.140
  619.6 7.6 convolution_add_fusion.7
  627.3 44.6 %reduce-scatter.9.cloned.1.call-done = f32[128,2048]{1,0:T(8,128)} async-done(((f32[512,2048]{1,0:T(8,128)}), f32[128,2048]{1,0:T(8,128)}) %reduce-scatter.9.cloned.1.call-update) | async-done | bytes 1048592 | tf_op jit(solution)/shard_map/reduce_scatter | solution.py:226
  677.7 20.0 all-gather.11.cloned.1.call-done
  697.7 6.2 multiply_reduce_fusion.4
  716.1 201.9 %while.98 = (s32[]{:T(128)}, f32[8,65,64]{1,2,0:T(8,128)S(1)}, f32[32,8,16,64]{3,2,1,0:T(8,128)}, f32[32,8,16]{2,1,0:T(8,128)}, f32[32,8,16,64]{3,2,1,0:T(8,128)}, /*index=5*/f32[32,8,16,64]{3,2,1,0:T(8,128)}) while((s32[]{:T(128)}, f32[8,65,64]{1,2,0:T(8,128)S(1)}, f32[32,8,16,64]{3,2,1,0:T(8,128)}, ...), condition=%wide.region_21.22_spmd.clone.clone, body=%wide.region_20.21_spmd.clone.sunk.clone | while | flops 48552844 | bytes 1615035 | solution.py:100
  918.0 69.7 %while.94 = (s32[]{:T(128)}, f32[8,65,64]{1,2,0:T(8,128)S(1)}, f32[8,65,65]{2,1,0:T(8,128)S(1)}, f32[8,65,64]{1,2,0:T(8,128)S(1)}) while((s32[]{:T(128)}, f32[8,65,64]{1,2,0:T(8,128)S(1)}, f32[8,65,65]{2,1,0:T(8,128)S(1)}, f32[8,65,64]{1,2,0:T(8,128)S(1)}) %tuple.220), condition=%wide.region_23.24_spmd.clone, body=%wide.region_22.23_spmd.sunk.clone | while | flops 25991680 | bytes 1067133 | solution.py:258
  920.0 8.4 collective-permute-done.1
  930.3 8.0 collective-permute-done.1
  940.2 7.6 collective-permute-done.1
  949.7 7.9 collective-permute-done.1
  959.4 7.9 collective-permute-done.1
  969.2 8.5 collective-permute-done.1
  979.6 8.1 collective-permute-done.1
  987.8 335.0 %while.95 = (s32[]{:T(128)}, f32[8,65,64]{1,2,0:T(8,128)S(1)}, bf16[32,8,16,64]{3,2,1,0:T(8,128)(2,1)S(1)}, bf16[32,8,16,64]{3,2,1,0:T(8,128)(2,1)}, bf16[32,8,1...) while((s32[]{:T(128)}, f32[8,65,64]{1,2,0:T(8,128)S(1)}, ...), condition=%wide.region_27.28_spmd.clone, body=%wide.region_24.27_spmd.sunk.clone | while | flops 52939520 | bytes 3343009 | solution.py:82
  1345.7 7.2 convolution_convert_fusion.9
  1353.0 8.2 convolution_convert_fusion.2
  1389.6 36.2 %all-reduce.10 = (bf16[2048,8]{0,1:T(8,128)(2,1)S(1)}, bf16[8]{0:T(256)(128)(2,1)S(1)}, bf16[8]{0:T(256)(128)(2,1)S(1)}, bf16[512]{0:T(512)(128)(2,1)S(1)}, bf16[512]{0:T(512)(128)(2,1)S(1)}) all-reduce(bf16[2048,8]{0,1:T(8,128)(2,1)S(1)} %convolution_convert_fusion.10, ...), channel_id=1, replica_groups=mesh['seq'=8,'head'=4] {'seq'}, use_global_device_ids=true, to_apply=%region_36.37 | all-reduce | flops 17424 | bytes 69696 | tf_op jit(solution)/shard_map/psum | solution.py:299
  1430.1 42.8 %all-reduce.7 = (f32[2048]{0:T(1024)}, f32[2048]{0:T(1024)}) all-reduce(f32[2048]{0:T(1024)S(1)} %get-tuple-element.720, f32[2048]{0:T(1024)S(1)} %get-tuple-element.715), channel_id=1, replica_groups=mesh['seq'=8,'head'=4] {'seq','head'}, use_global_device_ids=true, to_apply=%region_31.32 | all-reduce | flops 4096 | bytes 32768 | tf_op jit(solution)/shard_map/psum | solution.py:310
  1476.0 770.8 %all-reduce.14.cloned.1.call-done = (bf16[2048,512]{1,0:T(8,128)(2,1)}, bf16[2048,512]{1,0:T(8,128)(2,1)}, bf16[2048,512]{1,0:T(8,128)(2,1)}, bf16[2048,512]{1,0...) async-done(((bf16[2048,512]{1,0:T(8,128)(2,1)}, ...) | async-done | bytes 27460624 | tf_op jit(solution)/shard_map/psum | solution.py:295
  (1807 shorter events, 1133.7 us)
Async XLA Ops:
  7.2 508.6 %copy-start = (bf16[512,2048]{1,0:T(8,128)(2,1)S(1)}, bf16[512,2048]{1,0:T(8,128)(2,1)}, u32[]{:S(2)}) copy-start(bf16[512,2048]{1,0:T(8,128)(2,1)} %param.44) | copy-start | bytes 6291460
  7.3 28.9 %all-gather.5.cloned.1.call-start = ((), (), s32[]{:S(2)}) async-start(), calls=%async_computation.4 | async-start | bytes 2621440 | tf_op jit(solution)/shard_map/all_gather | solution.py:154
  10.7 541.9 %reduce-scatter.5.cloned.1.call-start = ((), (), s32[]{:S(2)}) async-start(), calls=%async_computation.5 | async-start | bytes 2621440 | tf_op jit(solution)/shard_map/reduce_scatter | solution.py:196
  232.7 9.6 collective-permute-start
  243.6 9.7 collective-permute-start
  254.7 8.8 collective-permute-start
  264.9 9.3 collective-permute-start
  275.6 9.4 collective-permute-start
  286.3 9.4 collective-permute-start
  297.0 9.4 collective-permute-start
  518.4 35.5 %copy-start.31 = (f32[2048]{0:T(1024)S(1)}, f32[2048]{0:T(1024)}, u32[]{:S(2)}) copy-start(f32[2048]{0:T(1024)} %param.45) | copy-start | bytes 24580
  518.4 60.4 %all-gather.7.cloned.1.call-start = ((), (), s32[]{:S(2)}) async-start(), calls=%async_computation.6 | async-start | bytes 2621440 | tf_op jit(solution)/shard_map/all_gather | solution.py:206
  556.0 46.9 %all-gather.9.cloned.1.call-start = ((), (), s32[]{:S(2)}) async-start(), calls=%async_computation.8 | async-start | bytes 2621440 | tf_op jit(solution)/shard_map/all_gather | solution.py:155
  556.6 115.3 %reduce-scatter.9.cloned.1.call-start = ((), (), s32[]{:S(2)}) async-start(), calls=%async_computation.9 | async-start | bytes 5242880 | tf_op jit(solution)/shard_map/reduce_scatter | solution.py:226
  627.2 44.7 %copy-start.5 = (bf16[128,2048]{1,0:T(8,128)(2,1)S(1)}, bf16[128,2048]{1,0:T(8,128)(2,1)}, u32[]{:S(2)}) copy-start(bf16[128,2048]{1,0:T(8,128)(2,1)} %reduce-scatter.5.cloned.1.call-done) | copy-start | bytes 1572868
  627.2 70.5 %all-gather.11.cloned.1.call-start = ((), (), s32[]{:S(2)}) async-start(), calls=%async_computation.10 | async-start | bytes 2621440 | tf_op jit(solution)/shard_map/all_gather | solution.py:239
  674.9 753.7 %reduce-scatter.11.cloned.1.call-start = ((), (), s32[]{:S(2)}) async-start(), calls=%async_computation.11 | async-start | bytes 2621440 | tf_op jit(solution)/shard_map/reduce_scatter | solution.py:281
  918.0 69.7 %copy-start.4 = (bf16[32,8,16,64]{3,2,1,0:T(8,128)(2,1)S(1)}, bf16[32,8,16,64]{3,2,1,0:T(8,128)(2,1)}, u32[]{:S(2)}) copy-start(bf16[32,8,16,64]{3,2,1,0:T(8,128)(2,1)} %copy-done.3) | copy-start | bytes 1572868
  918.7 9.7 collective-permute-start.1
  929.0 9.3 collective-permute-start.1
  938.9 8.9 collective-permute-start.1
  948.4 9.2 collective-permute-start.1
  958.1 9.2 collective-permute-start.1
  967.9 9.8 collective-permute-start.1
  978.3 9.4 collective-permute-start.1
  1344.4 128.5 %reduce-scatter.7.cloned.1.call-start = ((), (), s32[]{:S(2)}) async-start(), calls=%async_computation.7 | async-start | bytes 2621440 | tf_op jit(solution)/shard_map/reduce_scatter | solution.py:212
  1352.9 893.9 %all-reduce.14.cloned.1.call-start = ((), (), s32[]{:S(2)}) async-start(), calls=%async_computation.12 | async-start | bytes 55054336 | tf_op jit(solution)/shard_map/psum | solution.py:295
  1387.2 41.5 %copy-start.32 = (f32[2048]{0:T(1024)S(1)}, f32[2048]{0:T(1024)}, u32[]{:S(2)}) copy-start(f32[2048]{0:T(1024)} %param.32) | copy-start | bytes 24580
  1387.2 41.5 %copy-start.34 = (f32[128]{0:T(128)S(1)}, f32[128]{0:T(128)}, u32[]{:S(2)}) copy-start(f32[128]{0:T(128)} %copy-done.33) | copy-start | bytes 1540
  1387.2 85.7 %copy-start.6 = (bf16[128,2048]{1,0:T(8,128)(2,1)S(1)}, bf16[128,2048]{1,0:T(8,128)(2,1)}, u32[]{:S(2)}) copy-start(bf16[128,2048]{1,0:T(8,128)(2,1)} %reduce-scatter.5.cloned.1.call-done) | copy-start | bytes 1572868
  1387.2 85.7 %copy-start.8 = (f32[128,2048]{1,0:T(8,128)S(1)}, f32[128,2048]{1,0:T(8,128)}, u32[]{:S(2)}) copy-start(f32[128,2048]{1,0:T(8,128)} %reduce-scatter.9.cloned.1.call-done) | copy-start | bytes 3145732
  1387.2 85.7 %copy-start.12 = (bf16[128,2048]{1,0:T(8,128)(2,1)S(1)}, bf16[128,2048]{1,0:T(8,128)(2,1)}, u32[]{:S(2)}) copy-start(bf16[128,2048]{1,0:T(8,128)(2,1)} %param.49) | copy-start | bytes 1572868
  (47 other events, 331.7 us)
Sparse Core Ops, SparseCore 0:
  10.9 25.2 all-gather.4
  518.5 34.0 reduce-scatter.4
  556.1 22.5 all-gather.6
  580.2 22.5 all-gather.8
  627.3 44.4 reduce-scatter.8
  675.0 22.5 all-gather.10
  1344.5 33.6 reduce-scatter.10
  1381.4 31.4 reduce-scatter.6
  1421.0 825.7 all-reduce.13
where the time goes:
time: 2320 us; the launch traced here: 2290 us
  waiting for transfers between devices  1010 us (44%)
  matrix products  658 us (28%)
  local copies, waits for them, and re-layouts  380 us (16%)
  blocking collectives  91.2 us (4%)
  other arithmetic  81.4 us (4%)
  starting transfers between devices  42.1 us (2%)
    psum x1, waiting for transfers between devices, body(): lax.psum(query_grad.astype(jnp.bfloat16), 'seq').astype(jnp.float32)  771 us
    squeeze x256, local copies, waits for them, and re-layouts, segment_map(): lax.scan(turn, (identity, zero_state), (key_blocks, value_blocks, rate_bl...  213 us
    dot_general x128, matrix products, inner_block(): jnp.einsum('hmi,hio->hmo', key_aug, inner_state, precision=HIGHEST)  90.1 us
    ppermute x14, waiting for transfers between devices, passed_along(): return lax.ppermute(shard, axis, pairs)  89.2 us
    dot_general x64, matrix products, step_matrix_of(): jnp.einsum('hni,hnj->hij', weighted_keys, key_aug, precision=HIGHEST)  53.1 us
    dot_general x96, matrix products, inner_block(): jnp.einsum('hni,hno->hio', key_aug * rate_block[:, :, None], errors, prec...  52.9 us
    dot_general x32, matrix products, turn(): jnp.einsum('hni,hno->hio', weighted_keys, value_block - key_block, precis...  47.8 us
  transfers between devices with their start and end apart: 23, of which 21 were waited for; matrix products, arithmetic and copies ran while one was open for 3% of the time, Pallas kernels for 0%

commit v1 on v0

--- a/solution.py
+++ b/solution.py
@@ -1,3 +1,4 @@
+import functools
 import jax
 import jax.numpy as jnp
 from jax import lax
@@ -6,6 +7,13 @@
 MB = 16
 HIGHEST = lax.Precision.HIGHEST
 EPSILON = 1e-06
+
+
+def scenes_supply(state, axis_name):
+    return jnp.sum(lax.all_gather(state, axis_name), axis=0)
+
+
+_hold_task = functools.partial(scenes_supply, axis_name="seq")
 
 
 def passed_along(shard, axis, by):
@@ -292,7 +300,7 @@
         scaled_in - unit_in * jnp.mean(scaled_in * unit_in, axis=-1, keepdims=True)
     )
     summed = (
-        lax.psum(query_grad.astype(jnp.bfloat16), "seq").astype(jnp.float32),
+        _hold_task(query_grad.astype(jnp.bfloat16)).astype(jnp.float32),
         lax.psum(key_grad.astype(jnp.bfloat16), "seq").astype(jnp.float32),
         lax.psum(value_grad.astype(jnp.bfloat16), "seq").astype(jnp.float32),
         lax.psum(gate_grad.astype(jnp.bfloat16), "seq").astype(jnp.float32),

time: 2320 us -> 2470 us (1.065)
  waiting for transfers between devices: 1010 us -> 1150 us
    all_gather x0 -> x1, waiting for transfers between devices: none -> 194 us  [scenes_supply(): return jnp.sum(lax.all_gather(state, axis_name), axis=0)]
    psum x1, waiting for transfers between devices: 771 us -> 709 us  [body(): lax.psum(key_grad.astype(jnp.bfloat16), 'seq').astype(jnp.float32)]
  transfers between devices with their start and end apart: 23 -> 24, of which waited for: 21 -> 22; matrix products, arithmetic and copies ran while one was open for 3% -> 4% of each run, Pallas kernels for 0% -> 0%
where the time goes in v1:
time: 2470 us; the launch traced here: 2440 us
  waiting for transfers between devices  1150 us (47%)
  matrix products  658 us (27%)
  local copies, waits for them, and re-layouts  379 us (15%)
  other arithmetic  93.9 us (4%)
  blocking collectives  91.9 us (4%)
  starting transfers between devices  42 us (2%)
    psum x1, waiting for transfers between devices, body(): lax.psum(key_grad.astype(jnp.bfloat16), 'seq').astype(jnp.float32)  709 us
    squeeze x256, local copies, waits for them, and re-layouts, segment_map(): lax.scan(turn, (identity, zero_state), (key_blocks, value_blocks, rate_bl...  213 us
    all_gather x1, waiting for transfers between devices, scenes_supply(): return jnp.sum(lax.all_gather(state, axis_name), axis=0)  194 us
    dot_general x128, matrix products, inner_block(): jnp.einsum('hmi,hio->hmo', key_aug, inner_state, precision=HIGHEST)  90.1 us
    ppermute x14, waiting for transfers between devices, passed_along(): return lax.ppermute(shard, axis, pairs)  89.3 us
    dot_general x64, matrix products, step_matrix_of(): jnp.einsum('hni,hnj->hij', weighted_keys, key_aug, precision=HIGHEST)  53.1 us
    dot_general x96, matrix products, inner_block(): jnp.einsum('hni,hno->hio', key_aug * rate_block[:, :, None], errors, prec...  52.8 us
  transfers between devices with their start and end apart: 24, of which 22 were waited for; matrix products, arithmetic and copies ran while one was open for 4% of the time, Pallas kernels for 0%

profile of v1, /device:TPU:0, one launch (start us, length us, event | category | flops | bytes accessed | tf_op | source)
XLA Modules:
  0.0 2435.2 jit_solution(8103800803931328120)
XLA Ops:
  11.3 24.9 %all-gather.7.cloned.1.call-done = bf16[512,2048]{1,0:T(8,128)(2,1)} async-done(((bf16[128,2048]{1,0:T(8,128)(2,1)}), bf16[512,2048]{1,0:T(8,128)(2,1)}) %all-gather.7.cloned.1.call-update) | async-done | bytes 2097168 | tf_op jit(solution)/shard_map/all_gather | solution.py:162
  67.1 164.1 %while.97 = (s32[]{:T(128)}, f32[8,65,65]{2,1,0:T(8,128)S(1)}, f32[8,65,64]{1,2,0:T(8,128)S(1)}, f32[32,8,16,64]{3,2,1,0:T(8,128)}, f32[32,8,16]{2,1,0:T(8,128)}, /*index=5*/f32[32,8,16,64]{3,2,1,0:T(8,128)}) while((s32[]{:T(128)}, f32[8,65,65]{2,1,0:T(8,128)S(1)}, f32[8,65,64]{1,2,0:T(8,128)S(1)}, ...), condition=%wide.region_2.3_spmd.clone.clone, body=%wide.region_1.2_spmd.clone.sunk.clone | while | flops 65335404 | bytes 1942347 | solution.py:60
  231.3 75.0 %while.93 = (s32[]{:T(128)}, f32[8,65,64]{1,2,0:T(8,128)S(1)}, pred[]{:T(512)}, f32[8,65,65]{2,1,0:T(8,128)S(1)}, f32[8,65,64]{1,2,0:T(8,128)S(1)}, /*index=5*/f32[8,65,64]{1,2,0:T(8,128)S(1)}) while((s32[]{:T(128)}, f32[8,65,64]{1,2,0:T(8,128)S(1)}, pred[]{:T(512)}, f32[8,65,65]{2,1,0:T(8,128)S(1)}, f32[8,65,64]{1,2,0:T(8,128)S(1)}, ...), condition=%wide.region_4.5_spmd.clone, body=%wide.region_3.4_spmd.sunk.clone | while | flops 26024960 | bytes 1466510 | solution.py:190
  235.9 6.3 collective-permute-done
  306.3 189.6 %while.96 = (s32[]{:T(128)}, f32[8,65,64]{1,2,0:T(8,128)S(1)}, f32[32,8,16,64]{3,2,1,0:T(8,128)}, f32[32,8,65,64]{2,3,1,0:T(8,128)}, f32[32,8,16,64]{3,2,1,0:T(8...) while((s32[]{:T(128)}, f32[8,65,64]{1,2,0:T(8,128)S(1)}, ...), condition=%wide.region_6.7_spmd.clone.clone, body=%wide.region_5.6_spmd.clone.sunk.clone | while | flops 22418560 | bytes 1732721 | solution.py:90
  519.3 34.2 %reduce-scatter.5.cloned.1.call-done = bf16[128,2048]{1,0:T(8,128)(2,1)} async-done(((bf16[512,2048]{1,0:T(8,128)(2,1)}), bf16[128,2048]{1,0:T(8,128)(2,1)}) %reduce-scatter.5.cloned.1.call-update) | async-done | bytes 524304 | tf_op jit(solution)/shard_map/reduce_scatter | solution.py:204
  557.4 22.1 all-gather.9.cloned.1.call-done
  579.5 8.1 fusion.139
  587.6 7.7 fusion.138
  595.3 8.4 all-gather.11.cloned.1.call-done
  603.7 10.3 multiply_convert_fusion
  613.9 6.4 fusion.140
  620.4 7.6 convolution_add_fusion.7
  628.0 44.6 %reduce-scatter.9.cloned.1.call-done = f32[128,2048]{1,0:T(8,128)} async-done(((f32[512,2048]{1,0:T(8,128)}), f32[128,2048]{1,0:T(8,128)}) %reduce-scatter.9.cloned.1.call-update) | async-done | bytes 1048592 | tf_op jit(solution)/shard_map/reduce_scatter | solution.py:234
  678.5 20.0 all-gather.13.cloned.1.call-done
  716.8 201.9 %while.98 = (s32[]{:T(128)}, f32[8,65,64]{1,2,0:T(8,128)S(1)}, f32[32,8,16,64]{3,2,1,0:T(8,128)}, f32[32,8,16]{2,1,0:T(8,128)}, f32[32,8,16,64]{3,2,1,0:T(8,128)}, /*index=5*/f32[32,8,16,64]{3,2,1,0:T(8,128)}) while((s32[]{:T(128)}, f32[8,65,64]{1,2,0:T(8,128)S(1)}, f32[32,8,16,64]{3,2,1,0:T(8,128)}, ...), condition=%wide.region_21.22_spmd.clone.clone, body=%wide.region_20.21_spmd.clone.sunk.clone | while | flops 48552844 | bytes 1615035 | solution.py:108
  918.8 69.7 %while.94 = (s32[]{:T(128)}, f32[8,65,64]{1,2,0:T(8,128)S(1)}, f32[8,65,65]{2,1,0:T(8,128)S(1)}, f32[8,65,64]{1,2,0:T(8,128)S(1)}) while((s32[]{:T(128)}, f32[8,65,64]{1,2,0:T(8,128)S(1)}, f32[8,65,65]{2,1,0:T(8,128)S(1)}, f32[8,65,64]{1,2,0:T(8,128)S(1)}) %tuple.220), condition=%wide.region_23.24_spmd.clone, body=%wide.region_22.23_spmd.sunk.clone | while | flops 25991680 | bytes 1067133 | solution.py:266
  920.7 8.4 collective-permute-done.1
  931.0 8.0 collective-permute-done.1
  940.9 7.6 collective-permute-done.1
  950.4 7.9 collective-permute-done.1
  960.2 7.9 collective-permute-done.1
  970.0 8.5 collective-permute-done.1
  980.4 8.1 collective-permute-done.1
  988.5 334.8 %while.95 = (s32[]{:T(128)}, f32[8,65,64]{1,2,0:T(8,128)S(1)}, bf16[32,8,16,64]{3,2,1,0:T(8,128)(2,1)S(1)}, bf16[32,8,16,64]{3,2,1,0:T(8,128)(2,1)}, bf16[32,8,1...) while((s32[]{:T(128)}, f32[8,65,64]{1,2,0:T(8,128)S(1)}, ...), condition=%wide.region_27.28_spmd.clone, body=%wide.region_24.27_spmd.sunk.clone | while | flops 52939520 | bytes 3343009 | solution.py:90
  1343.5 7.2 convolution_convert_fusion.9
  1350.8 8.2 convolution_convert_fusion.2
  1387.6 36.1 %all-reduce.10 = (bf16[2048,8]{0,1:T(8,128)(2,1)S(1)}, bf16[8]{0:T(256)(128)(2,1)S(1)}, bf16[8]{0:T(256)(128)(2,1)S(1)}, bf16[512]{0:T(512)(128)(2,1)S(1)}, bf16[512]{0:T(512)(128)(2,1)S(1)}) all-reduce(bf16[2048,8]{0,1:T(8,128)(2,1)S(1)} %convolution_convert_fusion.10, ...), channel_id=1, replica_groups=mesh['seq'=8,'head'=4] {'seq'}, use_global_device_ids=true, to_apply=%region_36.37 | all-reduce | flops 17424 | bytes 69696 | tf_op jit(solution)/shard_map/psum | solution.py:307
  1428.0 43.6 %all-reduce.7 = (f32[2048]{0:T(1024)}, f32[2048]{0:T(1024)}) all-reduce(f32[2048]{0:T(1024)S(1)} %get-tuple-element.720, f32[2048]{0:T(1024)S(1)} %get-tuple-element.715), channel_id=1, replica_groups=mesh['seq'=8,'head'=4] {'seq','head'}, use_global_device_ids=true, to_apply=%region_31.32 | all-reduce | flops 4096 | bytes 32768 | tf_op jit(solution)/shard_map/psum | solution.py:318
  1474.7 709.3 %all-reduce.14.cloned.1.call-done = (bf16[2048,512]{1,0:T(8,128)(2,1)}, bf16[2048,512]{1,0:T(8,128)(2,1)}, bf16[2048,512]{1,0:T(8,128)(2,1)}, bf16[8,65,64]{2,0,...) async-done(((bf16[2048,512]{1,0:T(8,128)(2,1)}, bf16[2048,512]{1,0:T(8,128)(2,1)}, ...) | async-done | bytes 25363472 | tf_op jit(solution)/shard_map/psum | solution.py:304
  2219.3 194.1 %all-gather.15.cloned.1.call-done = bf16[16384,512]{1,0:T(8,128)(2,1)} async-done(((bf16[2048,512]{1,0:T(8,128)(2,1)}), bf16[16384,512]{1,0:T(8,128)(2,1)}) %all-gather.15.cloned.1.call-update) | async-done | bytes 16777232 | tf_op jit(solution)/shard_map/all_gather | solution.py:13
  2413.4 10.7 reduce_sum.194
  (1811 shorter events, 1146.5 us)
Async XLA Ops:
  7.2 509.4 %copy-start = (bf16[512,2048]{1,0:T(8,128)(2,1)S(1)}, bf16[512,2048]{1,0:T(8,128)(2,1)}, u32[]{:S(2)}) copy-start(bf16[512,2048]{1,0:T(8,128)(2,1)} %param.44) | copy-start | bytes 6291460
  7.3 28.9 %all-gather.7.cloned.1.call-start = ((), (), s32[]{:S(2)}) async-start(), calls=%async_computation.4 | async-start | bytes 2621440 | tf_op jit(solution)/shard_map/all_gather | solution.py:162
  10.7 542.7 %reduce-scatter.5.cloned.1.call-start = ((), (), s32[]{:S(2)}) async-start(), calls=%async_computation.5 | async-start | bytes 2621440 | tf_op jit(solution)/shard_map/reduce_scatter | solution.py:204
  232.6 9.6 collective-permute-start
  243.6 9.7 collective-permute-start
  254.7 8.8 collective-permute-start
  264.8 9.3 collective-permute-start
  275.5 9.4 collective-permute-start
  286.2 9.4 collective-permute-start
  296.9 9.4 collective-permute-start
  519.2 60.3 %all-gather.9.cloned.1.call-start = ((), (), s32[]{:S(2)}) async-start(), calls=%async_computation.6 | async-start | bytes 2621440 | tf_op jit(solution)/shard_map/all_gather | solution.py:214
  556.8 46.9 %all-gather.11.cloned.1.call-start = ((), (), s32[]{:S(2)}) async-start(), calls=%async_computation.8 | async-start | bytes 2621440 | tf_op jit(solution)/shard_map/all_gather | solution.py:163
  557.4 115.3 %reduce-scatter.9.cloned.1.call-start = ((), (), s32[]{:S(2)}) async-start(), calls=%async_computation.9 | async-start | bytes 5242880 | tf_op jit(solution)/shard_map/reduce_scatter | solution.py:234
  628.0 44.7 %copy-start.5 = (bf16[128,2048]{1,0:T(8,128)(2,1)S(1)}, bf16[128,2048]{1,0:T(8,128)(2,1)}, u32[]{:S(2)}) copy-start(bf16[128,2048]{1,0:T(8,128)(2,1)} %reduce-scatter.5.cloned.1.call-done) | copy-start | bytes 1572868
  628.0 70.5 %all-gather.13.cloned.1.call-start = ((), (), s32[]{:S(2)}) async-start(), calls=%async_computation.10 | async-start | bytes 2621440 | tf_op jit(solution)/shard_map/all_gather | solution.py:247
  675.7 750.8 %reduce-scatter.11.cloned.1.call-start = ((), (), s32[]{:S(2)}) async-start(), calls=%async_computation.11 | async-start | bytes 2621440 | tf_op jit(solution)/shard_map/reduce_scatter | solution.py:289
  918.8 69.7 %copy-start.4 = (bf16[32,8,16,64]{3,2,1,0:T(8,128)(2,1)S(1)}, bf16[32,8,16,64]{3,2,1,0:T(8,128)(2,1)}, u32[]{:S(2)}) copy-start(bf16[32,8,16,64]{3,2,1,0:T(8,128)(2,1)} %copy-done.3) | copy-start | bytes 1572868
  919.4 9.7 collective-permute-start.1
  929.7 9.3 collective-permute-start.1
  939.6 8.9 collective-permute-start.1
  949.1 9.2 collective-permute-start.1
  958.9 9.2 collective-permute-start.1
  968.7 9.8 collective-permute-start.1
  979.1 9.4 collective-permute-start.1
  1342.2 129.4 %reduce-scatter.7.cloned.1.call-start = ((), (), s32[]{:S(2)}) async-start(), calls=%async_computation.7 | async-start | bytes 2621440 | tf_op jit(solution)/shard_map/reduce_scatter | solution.py:220
  1350.7 833.3 %all-reduce.14.cloned.1.call-start = ((), (), s32[]{:S(2)}) async-start(), calls=%async_computation.13 | async-start | bytes 50860032 | tf_op jit(solution)/shard_map/psum | solution.py:304
  1382.4 1031.0 %all-gather.15.cloned.1.call-start = ((), (), s32[]{:S(2)}) async-start(), calls=%async_computation.12 | async-start | bytes 18874368 | tf_op jit(solution)/shard_map/all_gather | solution.py:13
  1385.1 41.4 %copy-start.32 = (f32[2048]{0:T(1024)S(1)}, f32[2048]{0:T(1024)}, u32[]{:S(2)}) copy-start(f32[2048]{0:T(1024)} %param.32) | copy-start | bytes 24580
  1385.1 41.4 %copy-start.34 = (f32[128]{0:T(128)S(1)}, f32[128]{0:T(128)}, u32[]{:S(2)}) copy-start(f32[128]{0:T(128)} %copy-done.33) | copy-start | bytes 1540
  1385.1 86.4 %copy-start.6 = (bf16[128,2048]{1,0:T(8,128)(2,1)S(1)}, bf16[128,2048]{1,0:T(8,128)(2,1)}, u32[]{:S(2)}) copy-start(bf16[128,2048]{1,0:T(8,128)(2,1)} %reduce-scatter.5.cloned.1.call-done) | copy-start | bytes 1572868
  1385.1 86.4 %copy-start.8 = (f32[128,2048]{1,0:T(8,128)S(1)}, f32[128,2048]{1,0:T(8,128)}, u32[]{:S(2)}) copy-start(f32[128,2048]{1,0:T(8,128)} %reduce-scatter.9.cloned.1.call-done) | copy-start | bytes 3145732
  1385.1 86.4 %copy-start.12 = (bf16[128,2048]{1,0:T(8,128)(2,1)S(1)}, bf16[128,2048]{1,0:T(8,128)(2,1)}, u32[]{:S(2)}) copy-start(bf16[128,2048]{1,0:T(8,128)(2,1)} %param.49) | copy-start | bytes 1572868
  (48 other events, 398.4 us)
Sparse Core Ops, SparseCore 0:
  10.9 25.2 all-gather.6
  519.3 34.0 reduce-scatter.4
  556.9 22.5 all-gather.8
  581.0 22.5 all-gather.10
  628.1 44.4 reduce-scatter.8
  675.8 22.5 all-gather.12
  1342.3 33.5 reduce-scatter.10
  1379.2 31.4 reduce-scatter.6
  1418.1 765.9 all-reduce.13
  2186.8 226.4 all-gather.14
